TPU v7x, 32 devices: a whole 2x2x4 slice. The times are simulated.
32 devices in a mesh: dom: 32 (over z, y, x, core).
Axes of the slice: x: 2, y: 2, z: 4, core: 2. Of those that a mesh axis runs over, the one named last changes fastest.
Arguments:
- vectors: bfloat16 [64, 131072], P(None, 'dom')
- diag_tiles: bfloat16 [1024, 128, 128], P('dom'), as said below
- pair_tiles: bfloat16 [3072, 2, 128, 128], P('dom'), as said below
- halo_tiles: bfloat16 [1024, 128, 128], P('dom'), as said below
- halo_rows: int32 [32, 32], P('dom'), may hold values from 1 to 31, as said below
- pair_index: int32 [32, 96, 2], P('dom'), may hold values from 0 to 31, as said below
- pair_count: int32 [32], P('dom'), may hold values from 24 to 96, as said below
Outputs:
- basis: bfloat16 [64, 131072], P(None, 'dom')
- ritz: float32 [64, 64], replicated
Inputs may be any that keep to these rules, and one draw needn't show every extreme that they name: `diag_tiles`: each tile is symmetric. `pair_tiles`: entry [j, 1] is the transpose of entry [j, 0]. `halo_tiles`: entry d * 32 + p is the transpose of entry p * 32 + d. `halo_rows`: no entry is a multiple of 4. `pair_index`: the 96 entries of a partition are distinct pairs (r, c) with r < c. The first pair_count[d] entries of pair_index[d] are live; some partition has 96.
All inputs are finite; a program needn't handle non-finite values.
Results may differ from a plain program's by a relative error of at most 0.023.
Values may be sent and summed in bfloat16 or wider, within the bound.
A program may use at most 128 MiB of HBM per device.

v0:
```python
import jax
import jax.numpy as jnp
from jax import lax
from jax.sharding import PartitionSpec as P

DEGREE = 4
first_centre = -0.5


def local(vectors, diag_tiles, pair_tiles, halo_tiles, halo_rows, pair_index, pair_count):
    vec_width = vectors.shape[0]
    tile_size = diag_tiles.shape[1]
    blocks = diag_tiles.shape[0]
    peers = lax.axis_size("dom")
    total_rows = tile_size * blocks * peers
    block_iota = jnp.arange(blocks)
    row_ids = pair_index[0, :, 0]
    col_ids = pair_index[0, :, 1]
    live_mask = (jnp.arange(pair_index.shape[1]) < pair_count[0]).astype(jnp.float32)
    onehot_first = (row_ids[:, None] == block_iota[None, :]).astype(jnp.float32) * live_mask[
        :, None
    ]
    onehot_second = (col_ids[:, None] == block_iota[None, :]).astype(jnp.float32) * live_mask[
        :, None
    ]
    send_rows = halo_rows[0]
    onehot_halo = (send_rows[:, None] == block_iota[None, :]).astype(jnp.float32)

    def halo_terms(arrived):
        products = jnp.einsum(
            "kpj,pij->kpi", arrived, halo_tiles, preferred_element_type=jnp.float32
        )
        return jnp.einsum("kpi,pr->kri", products, onehot_halo)

    def operator(current):
        blocked = current.reshape(vec_width, blocks, tile_size)
        outgoing = jnp.take(blocked, send_rows, axis=1)
        result = halo_terms(
            lax.all_to_all(outgoing, "dom", split_axis=1, concat_axis=1, tiled=True)
        )
        result = result + jnp.einsum(
            "krj,rij->kri", blocked, diag_tiles, preferred_element_type=jnp.float32
        )
        from_cols = jnp.take(blocked, col_ids, axis=1)
        from_rows = jnp.take(blocked, row_ids, axis=1)
        upper_terms = jnp.einsum(
            "kej,eij->kei", from_cols, pair_tiles[:, 0], preferred_element_type=jnp.float32
        )
        lower_terms = jnp.einsum(
            "kej,eji->kei", from_rows, pair_tiles[:, 0], preferred_element_type=jnp.float32
        )
        result = result + jnp.einsum("kei,er->kri", upper_terms, onehot_first)
        result = result + jnp.einsum("kei,er->kri", lower_terms, onehot_second)
        return result.reshape(vec_width, blocks * tile_size)

    def subspace_step(start, first, centre):
        previous = start
        current = (first - centre * start.astype(jnp.float32)).astype(jnp.bfloat16)
        for degree in range(DEGREE - 1):
            applied = operator(current)
            following = (
                2.0 * (applied - centre * current.astype(jnp.float32))
                - previous.astype(jnp.float32)
            ).astype(jnp.bfloat16)
            previous, current = (current, following)
        partial_value = jnp.dot(current, current.T, preferred_element_type=jnp.float32) / total_rows
        gram_matrix = lax.psum(partial_value, "dom")
        chol_lower = jnp.linalg.cholesky(gram_matrix)
        inverse = jax.scipy.linalg.solve_triangular(
            chol_lower, jnp.eye(vec_width, dtype=jnp.float32), lower=True
        )
        following = jnp.dot(
            inverse, current.astype(jnp.float32), precision=lax.Precision.HIGHEST
        ).astype(jnp.bfloat16)
        applied = operator(following)
        projected = (
            jnp.dot(following.astype(jnp.float32), applied.T, precision=lax.Precision.HIGHEST)
            / total_rows
        )
        return (following, applied, projected)

    first = operator(vectors)
    basis_one, image_one, partial_one = subspace_step(vectors, first, first_centre)
    mean_ritz = jnp.trace(lax.psum(partial_one, "dom")) / vec_width
    basis, image_two, partial_two = subspace_step(basis_one, image_one, mean_ritz - 1.0)
    ritz = lax.psum(partial_two, "dom")
    return (basis, ritz)


def solution(mesh):
    return jax.shard_map(
        local,
        mesh=mesh,
        in_specs=(
            P(None, "dom"),
            P("dom", None, None),
            P("dom", None, None, None),
            P("dom", None, None),
            P("dom", None),
            P("dom", None, None),
            P("dom"),
        ),
        out_specs=(P(None, "dom"), P()),
        check_vma=False,
    )
```

profile of v0, /device:TPU:0, one launch (start us, length us, event | category | flops | bytes accessed | tf_op | source)
XLA Modules:
  0.0 501.2 jit_solution(12377639445538355991)
XLA Ops:
  4.8 7.3 %all-to-all-start = ((bf16[64,32,128]{2,0,1:T(8,128)(2,1)}), bf16[64,32,128]{2,0,1:T(8,128)(2,1)S(1)}, u32[]{:S(2)}, u32[]{:S(2)}) async-start(bf16[64,32,128]{2,0,1:T(8,128)(2,1)} %select_bitcast_fusion.8), calls=%async_computation | async-start | bytes 1048576 | tf_op jit(solution)/shard_map/all_to_all | solution.py:39
  25.2 5.4 %fusion.72 = bf16[64,96,128]{2,0,1:T(8,128)(2,1)} fusion(bf16[96,64,128]{2,1,0:T(8,128)(2,1)S(1)} %copy-done.59, pred[96]{0:T(512)(128)(4,1)S(1)} %get-tuple-element.12, bf16[96,2,128,128]{3,2,1,0:T(8,128)(2,1)} %param.16), kind=kOutput, calls=%fused_computation.101 | convolution fusion | flops 202113024 | bytes 6291552 | tf_op jit(solution)/shard_map/kej,eij->kei/dot_general | solution.py:46
  40.6 6.1 %all-to-all-start.1 = ((bf16[64,32,128]{2,0,1:T(8,128)(2,1)}), bf16[64,32,128]{2,0,1:T(8,128)(2,1)}, u32[]{:S(2)}, u32[]{:S(2)}) async-start(bf16[64,32,128]{2,0,1:T(8,128)(2,1)} %select_bitcast_fusion.7), calls=%async_computation.1 | async-start | bytes 1048576 | tf_op jit(solution)/shard_map/all_to_all | solution.py:39
  57.1 5.3 %fusion.78 = bf16[64,96,128]{2,0,1:T(8,128)(2,1)} fusion(bf16[96,64,128]{2,1,0:T(8,128)(2,1)S(1)} %copy-done.60, pred[96]{0:T(512)(128)(4,1)S(1)} %get-tuple-element.12, bf16[96,2,128,128]{3,2,1,0:T(8,128)(2,1)} %param.16), kind=kOutput, calls=%fused_computation.103 | convolution fusion | flops 202113024 | bytes 6291552 | tf_op jit(solution)/shard_map/kej,eij->kei/dot_general | solution.py:46
  74.5 6.3 %all-to-all-start.2 = ((bf16[64,32,128]{2,0,1:T(8,128)(2,1)}), bf16[64,32,128]{2,0,1:T(8,128)(2,1)}, u32[]{:S(2)}, u32[]{:S(2)}) async-start(bf16[64,32,128]{2,0,1:T(8,128)(2,1)} %select_bitcast_fusion.6), calls=%async_computation.2 | async-start | bytes 1048576 | tf_op jit(solution)/shard_map/all_to_all | solution.py:39
  92.3 5.3 %fusion.84 = bf16[64,96,128]{2,0,1:T(8,128)(2,1)} fusion(bf16[96,64,128]{2,1,0:T(8,128)(2,1)S(1)} %copy-done.61, pred[96]{0:T(512)(128)(4,1)S(1)} %get-tuple-element.12, bf16[96,2,128,128]{3,2,1,0:T(8,128)(2,1)} %param.16), kind=kOutput, calls=%fused_computation.105 | convolution fusion | flops 202113024 | bytes 6291552 | tf_op jit(solution)/shard_map/kej,eij->kei/dot_general | solution.py:46
  111.4 6.3 %all-to-all-start.3 = ((bf16[64,32,128]{2,0,1:T(8,128)(2,1)}), bf16[64,32,128]{2,0,1:T(8,128)(2,1)}, u32[]{:S(2)}, u32[]{:S(2)}) async-start(bf16[64,32,128]{2,0,1:T(8,128)(2,1)} %select_bitcast_fusion.5), calls=%async_computation.3 | async-start | bytes 1048576 | tf_op jit(solution)/shard_map/all_to_all | solution.py:39
  125.2 5.3 %fusion.90 = bf16[64,96,128]{2,0,1:T(8,128)(2,1)} fusion(bf16[96,64,128]{2,1,0:T(8,128)(2,1)S(1)} %copy-done.56, pred[96]{0:T(512)(128)(4,1)S(1)} %get-tuple-element.12, bf16[96,2,128,128]{3,2,1,0:T(8,128)(2,1)} %param.16), kind=kOutput, calls=%fused_computation.107 | convolution fusion | flops 202113024 | bytes 6291552 | tf_op jit(solution)/shard_map/kej,eij->kei/dot_general | solution.py:46
  141.3 39.5 %psum.28 = f32[64,64]{0,1:T(8,128)S(1)} all-reduce(f32[64,64]{0,1:T(8,128)S(1)} %convolution_multiply_fusion.3), channel_id=1, replica_groups=mesh['dom'=32] {'dom'}, use_global_device_ids=true, to_apply=%region_0.3 | all-reduce | flops 4096 | bytes 32768 | tf_op jit(solution)/shard_map/psum | solution.py:67
  180.9 5.8 %cholesky.44 = f32[64,64]{1,0:T(8,128)S(1)} custom-call(f32[64,64]{1,0:T(8,128)S(1)} %fusion.301), custom_call_target="Cholesky" | custom-call | tf_op jit(solution)/shard_map/jit(cholesky)/cholesky | solution.py:68
  188.1 4.9 custom-call.6
  214.7 5.3 %fusion.96 = bf16[64,96,128]{2,0,1:T(8,128)(2,1)} fusion(bf16[96,64,128]{2,1,0:T(8,128)(2,1)S(1)} %copy-done.62, pred[96]{0:T(512)(128)(4,1)S(1)} %get-tuple-element.12, bf16[96,2,128,128]{3,2,1,0:T(8,128)(2,1)} %param.16), kind=kOutput, calls=%fused_computation.109 | convolution fusion | flops 202113024 | bytes 6291552 | tf_op jit(solution)/shard_map/kej,eij->kei/dot_general | solution.py:46
  227.0 40.7 %psum.29 = f32[64,64]{0,1:T(8,128)S(1)} all-reduce(f32[64,64]{0,1:T(8,128)S(1)} %convolution_multiply_fusion.2), channel_id=1, replica_groups=mesh['dom'=32] {'dom'}, use_global_device_ids=true, to_apply=%region_3.8 | all-reduce | flops 4096 | bytes 32768 | tf_op jit(solution)/shard_map/psum | solution.py:84
  276.4 4.6 all-to-all-start.5
  291.4 5.3 %fusion.102 = bf16[64,96,128]{2,0,1:T(8,128)(2,1)} fusion(bf16[96,64,128]{2,1,0:T(8,128)(2,1)S(1)} %copy-done.63, pred[96]{0:T(512)(128)(4,1)S(1)} %get-tuple-element.12, bf16[96,2,128,128]{3,2,1,0:T(8,128)(2,1)} %param.16), kind=kOutput, calls=%fused_computation.111 | convolution fusion | flops 202113024 | bytes 6291552 | tf_op jit(solution)/shard_map/kej,eij->kei/dot_general | solution.py:46
  308.7 6.1 %all-to-all-start.6 = ((bf16[64,32,128]{2,0,1:T(8,128)(2,1)}), bf16[64,32,128]{2,0,1:T(8,128)(2,1)}, u32[]{:S(2)}, u32[]{:S(2)}) async-start(bf16[64,32,128]{2,0,1:T(8,128)(2,1)} %select_bitcast_fusion.2), calls=%async_computation.6 | async-start | bytes 1048576 | tf_op jit(solution)/shard_map/all_to_all | solution.py:39
  326.3 5.3 %fusion.108 = bf16[64,96,128]{2,0,1:T(8,128)(2,1)} fusion(bf16[96,64,128]{2,1,0:T(8,128)(2,1)S(1)} %copy-done.64, pred[96]{0:T(512)(128)(4,1)S(1)} %get-tuple-element.12, bf16[96,2,128,128]{3,2,1,0:T(8,128)(2,1)} %param.16), kind=kOutput, calls=%fused_computation.113 | convolution fusion | flops 202113024 | bytes 6291552 | tf_op jit(solution)/shard_map/kej,eij->kei/dot_general | solution.py:46
  345.4 6.5 %all-to-all-start.7 = ((bf16[64,32,128]{2,0,1:T(8,128)(2,1)}), bf16[64,32,128]{2,0,1:T(8,128)(2,1)}, u32[]{:S(2)}, u32[]{:S(2)}) async-start(bf16[64,32,128]{2,0,1:T(8,128)(2,1)} %select_bitcast_fusion.1), calls=%async_computation.7 | async-start | bytes 1048576 | tf_op jit(solution)/shard_map/all_to_all | solution.py:39
  359.3 5.3 %fusion.114 = bf16[64,96,128]{2,0,1:T(8,128)(2,1)} fusion(bf16[96,64,128]{2,1,0:T(8,128)(2,1)S(1)} %copy-done.57, pred[96]{0:T(512)(128)(4,1)S(1)} %get-tuple-element.12, bf16[96,2,128,128]{3,2,1,0:T(8,128)(2,1)} %param.16), kind=kOutput, calls=%fused_computation.115 | convolution fusion | flops 202113024 | bytes 6291552 | tf_op jit(solution)/shard_map/kej,eij->kei/dot_general | solution.py:46
  375.4 39.2 %psum.30 = f32[64,64]{0,1:T(8,128)S(1)} all-reduce(f32[64,64]{0,1:T(8,128)S(1)} %convolution_multiply_fusion.1), channel_id=1, replica_groups=mesh['dom'=32] {'dom'}, use_global_device_ids=true, to_apply=%region_5.10 | all-reduce | flops 4096 | bytes 32768 | tf_op jit(solution)/shard_map/psum | solution.py:67
  414.7 5.8 %cholesky.55 = f32[64,64]{1,0:T(8,128)S(1)} custom-call(f32[64,64]{1,0:T(8,128)S(1)} %fusion.299), custom_call_target="Cholesky" | custom-call | tf_op jit(solution)/shard_map/jit(cholesky)/cholesky | solution.py:68
  421.9 4.9 custom-call.7
  448.5 5.3 %fusion.120 = bf16[64,96,128]{2,0,1:T(8,128)(2,1)} fusion(bf16[96,64,128]{2,1,0:T(8,128)(2,1)S(1)} %copy-done.58, pred[96]{0:T(512)(128)(4,1)S(1)} %get-tuple-element.12, bf16[96,2,128,128]{3,2,1,0:T(8,128)(2,1)} %param.16), kind=kOutput, calls=%fused_computation.117 | convolution fusion | flops 202113024 | bytes 6291552 | tf_op jit(solution)/shard_map/kej,eij->kei/dot_general | solution.py:46
  459.8 40.5 %psum.31 = f32[64,64]{0,1:T(8,128)S(1)} all-reduce(f32[64,64]{0,1:T(8,128)S(1)} %convolution_multiply_fusion), channel_id=1, replica_groups=mesh['dom'=32] {'dom'}, use_global_device_ids=true, to_apply=%region_6.11 | all-reduce | flops 4096 | bytes 32768 | tf_op jit(solution)/shard_map/psum | solution.py:86
  (277 shorter events, 225.5 us)
Async XLA Ops:
  0.6 20.7 %copy-start = (bf16[32,128,128]{2,1,0:T(8,128)(2,1)S(1)}, bf16[32,128,128]{2,1,0:T(8,128)(2,1)}, u32[]{:S(2)}) copy-start(bf16[32,128,128]{2,1,0:T(8,128)(2,1)} %param.15) | copy-start | bytes 3145732
  3.3 8.9 %copy-start.66 = (s32[1,96,2]{1,2,0:T(2,128)S(1)}, s32[1,96,2]{1,2,0:T(2,128)}, u32[]{:S(2)}) copy-start(s32[1,96,2]{1,2,0:T(2,128)} %param.19) | copy-start | bytes 2308
  4.8 25.8 %all-to-all-start = ((bf16[64,32,128]{2,0,1:T(8,128)(2,1)}), bf16[64,32,128]{2,0,1:T(8,128)(2,1)S(1)}, u32[]{:S(2)}, u32[]{:S(2)}) async-start(bf16[64,32,128]{2,0,1:T(8,128)(2,1)} %select_bitcast_fusion.8), calls=%async_computation | async-start | bytes 1048576 | tf_op jit(solution)/shard_map/all_to_all | solution.py:39
  23.1 2.1 copy-start.59
  25.2 5.4 %copy-start.1 = (bf16[32,128,128]{2,1,0:T(8,128)(2,1)S(1)}, bf16[32,128,128]{2,1,0:T(8,128)(2,1)}, u32[]{:S(2)}) copy-start(bf16[32,128,128]{2,1,0:T(8,128)(2,1)} %param.17) | copy-start | bytes 3145732
  40.6 21.9 %all-to-all-start.1 = ((bf16[64,32,128]{2,0,1:T(8,128)(2,1)}), bf16[64,32,128]{2,0,1:T(8,128)(2,1)}, u32[]{:S(2)}, u32[]{:S(2)}) async-start(bf16[64,32,128]{2,0,1:T(8,128)(2,1)} %select_bitcast_fusion.7), calls=%async_computation.1 | async-start | bytes 1048576 | tf_op jit(solution)/shard_map/all_to_all | solution.py:39
  55.0 2.1 copy-start.60
  74.5 23.2 %all-to-all-start.2 = ((bf16[64,32,128]{2,0,1:T(8,128)(2,1)}), bf16[64,32,128]{2,0,1:T(8,128)(2,1)}, u32[]{:S(2)}, u32[]{:S(2)}) async-start(bf16[64,32,128]{2,0,1:T(8,128)(2,1)} %select_bitcast_fusion.6), calls=%async_computation.2 | async-start | bytes 1048576 | tf_op jit(solution)/shard_map/all_to_all | solution.py:39
  87.3 3.0 copy-start.52
  101.3 2.1 copy-start.5
  111.4 21.9 %all-to-all-start.3 = ((bf16[64,32,128]{2,0,1:T(8,128)(2,1)}), bf16[64,32,128]{2,0,1:T(8,128)(2,1)}, u32[]{:S(2)}, u32[]{:S(2)}) async-start(bf16[64,32,128]{2,0,1:T(8,128)(2,1)} %select_bitcast_fusion.5), calls=%async_computation.3 | async-start | bytes 1048576 | tf_op jit(solution)/shard_map/all_to_all | solution.py:39
  121.2 2.1 copy-start.6
  121.2 2.1 copy-start.14
  194.8 74.2 %copy-start.2 = (bf16[64,4096]{1,0:T(8,128)(2,1)}, bf16[64,4096]{1,0:T(8,128)(2,1)S(1)}, u32[]{:S(2)}) copy-start(bf16[64,4096]{1,0:T(8,128)(2,1)S(1)} %convolution_convert_fusion.1) | copy-start | bytes 1572868
  200.3 19.6 %all-to-all-start.4 = ((bf16[64,32,128]{2,0,1:T(8,128)(2,1)}), bf16[64,32,128]{2,0,1:T(8,128)(2,1)}, u32[]{:S(2)}, u32[]{:S(2)}) async-start(bf16[64,32,128]{2,0,1:T(8,128)(2,1)} %select_bitcast_fusion.4), calls=%async_computation.4 | async-start | bytes 1048576 | tf_op jit(solution)/shard_map/all_to_all | solution.py:39
  276.4 20.3 %all-to-all-start.5 = ((bf16[64,32,128]{2,0,1:T(8,128)(2,1)}), bf16[64,32,128]{2,0,1:T(8,128)(2,1)}, u32[]{:S(2)}, u32[]{:S(2)}) async-start(bf16[64,32,128]{2,0,1:T(8,128)(2,1)} %select_bitcast_fusion.3), calls=%async_computation.5 | async-start | bytes 1048576 | tf_op jit(solution)/shard_map/all_to_all | solution.py:39
  308.7 23.0 %all-to-all-start.6 = ((bf16[64,32,128]{2,0,1:T(8,128)(2,1)}), bf16[64,32,128]{2,0,1:T(8,128)(2,1)}, u32[]{:S(2)}, u32[]{:S(2)}) async-start(bf16[64,32,128]{2,0,1:T(8,128)(2,1)} %select_bitcast_fusion.2), calls=%async_computation.6 | async-start | bytes 1048576 | tf_op jit(solution)/shard_map/all_to_all | solution.py:39
  321.3 3.0 copy-start.55
  335.3 2.1 copy-start.8
  345.4 22.1 %all-to-all-start.7 = ((bf16[64,32,128]{2,0,1:T(8,128)(2,1)}), bf16[64,32,128]{2,0,1:T(8,128)(2,1)}, u32[]{:S(2)}, u32[]{:S(2)}) async-start(bf16[64,32,128]{2,0,1:T(8,128)(2,1)} %select_bitcast_fusion.1), calls=%async_computation.7 | async-start | bytes 1048576 | tf_op jit(solution)/shard_map/all_to_all | solution.py:39
  355.3 2.1 copy-start.9
  355.3 2.1 copy-start.11
  428.6 30.0 %copy-start.17 = (bf16[64,4096]{1,0:T(8,128)(2,1)}, bf16[64,4096]{1,0:T(8,128)(2,1)S(1)}, u32[]{:S(2)}) copy-start(bf16[64,4096]{1,0:T(8,128)(2,1)S(1)} %convolution_convert_fusion) | copy-start | bytes 1572868
  434.2 19.6 %all-to-all-start.8 = ((bf16[64,32,128]{2,0,1:T(8,128)(2,1)}), bf16[64,32,128]{2,0,1:T(8,128)(2,1)}, u32[]{:S(2)}, u32[]{:S(2)}) async-start(bf16[64,32,128]{2,0,1:T(8,128)(2,1)} %select_bitcast_fusion), calls=%async_computation.8 | async-start | bytes 1048576 | tf_op jit(solution)/shard_map/all_to_all | solution.py:39
  (52 other events, 80.4 us)
where the time goes:
time: 510 us; the launch traced here: 501 us
  matrix products  165 us (32%)
  blocking collectives  160 us (31%)
  local copies, waits for them, and re-layouts  63.9 us (13%)
  other arithmetic  52.2 us (10%)
  starting transfers between devices  51.1 us (10%)
  waiting for transfers between devices  5.72 us (1%)
    psum x2, blocking collectives, subspace_step(): gram_matrix = lax.psum(partial_value, 'dom')  78.7 us
    all_to_all x9, starting transfers between devices, operator(): lax.all_to_all(outgoing, 'dom', split_axis=1, concat_axis=1, tiled=True)  51.1 us
    dot_general x9, matrix products, operator(): jnp.einsum('kej,eij->kei', from_cols, pair_tiles[:, 0], preferred_element...  48 us
    psum x1, blocking collectives, local(): mean_ritz = jnp.trace(lax.psum(partial_one, 'dom')) / vec_width  40.7 us
    psum x1, blocking collectives, local(): ritz = lax.psum(partial_two, 'dom')  40.5 us
    dot_general x9, matrix products, operator(): jnp.einsum('kej,eji->kei', from_rows, pair_tiles[:, 0], preferred_element...  38.6 us
    dot_general x9, matrix products, operator(): result = result + jnp.einsum('kei,er->kri', lower_terms, onehot_second)  18.7 us
    dot_general x9, matrix products, operator(): jnp.einsum('krj,rij->kri', blocked, diag_tiles, preferred_element_type=jn...  18.7 us
  transfers between devices with their start and end apart: 9, of which 2 were waited for; matrix products, arithmetic and copies ran while one was open for 28% of the time, Pallas kernels for 0%

commit v1 on v0

--- a/solution.py
+++ b/solution.py
@@ -83,7 +83,9 @@
     basis_one, image_one, partial_one = subspace_step(vectors, first, first_centre)
     mean_ritz = jnp.trace(lax.psum(partial_one, "dom")) / vec_width
     basis, image_two, partial_two = subspace_step(basis_one, image_one, mean_ritz - 1.0)
-    ritz = lax.psum(partial_two, "dom")
+    ritz = partial_two
+    for hop in (1, 2, 4, 8, 16):
+        ritz = ritz + lax.ppermute(ritz, "dom", [(dev, dev ^ hop) for dev in range(32)])
     return (basis, ritz)
 
 

time: 510 us -> 487 us (0.955)
  blocking collectives: 160 us -> 119 us
  waiting for transfers between devices: 5.72 us -> 15.6 us
  starting transfers between devices: 51.1 us -> 59 us
    psum x1 -> x0, blocking collectives: 40.5 us -> none  [local(): ritz = lax.psum(partial_two, 'dom')]
    ppermute x0 -> x5, waiting for transfers between devices: none -> 9.9 us  [local(): lax.ppermute(ritz, 'dom', [(dev, dev ^ hop) for dev in range(32)])]
    ppermute x0 -> x5, starting transfers between devices: none -> 7.93 us  [local(): lax.ppermute(ritz, 'dom', [(dev, dev ^ hop) for dev in range(32)])]
  transfers between devices with their start and end apart: 9 -> 14, of which waited for: 2 -> 7; matrix products, arithmetic and copies ran while one was open for 28% -> 29% of each run, Pallas kernels for 0% -> 0%
where the time goes in v1:
time: 487 us; the launch traced here: 479 us
  matrix products  165 us (34%)
  blocking collectives  119 us (24%)
  local copies, waits for them, and re-layouts  63.9 us (13%)
  starting transfers between devices  59 us (12%)
  other arithmetic  52.1 us (11%)
  waiting for transfers between devices  15.6 us (3%)
    psum x2, blocking collectives, subspace_step(): gram_matrix = lax.psum(partial_value, 'dom')  78.7 us
    all_to_all x9, starting transfers between devices, operator(): lax.all_to_all(outgoing, 'dom', split_axis=1, concat_axis=1, tiled=True)  51.1 us
    dot_general x9, matrix products, operator(): jnp.einsum('kej,eij->kei', from_cols, pair_tiles[:, 0], preferred_element...  48.1 us
    psum x1, blocking collectives, local(): mean_ritz = jnp.trace(lax.psum(partial_one, 'dom')) / vec_width  40.7 us
    dot_general x9, matrix products, operator(): jnp.einsum('kej,eji->kei', from_rows, pair_tiles[:, 0], preferred_element...  38.5 us
    dot_general x9, matrix products, operator(): result = result + jnp.einsum('kei,er->kri', lower_terms, onehot_second)  18.8 us
    dot_general x9, matrix products, operator(): jnp.einsum('krj,rij->kri', blocked, diag_tiles, preferred_element_type=jn...  18.7 us
    gather x9, local copies, waits for them, and re-layouts, operator(): from_cols = jnp.take(blocked, col_ids, axis=1)  17.7 us
  transfers between devices with their start and end apart: 14, of which 7 were waited for; matrix products, arithmetic and copies ran while one was open for 29% of the time, Pallas kernels for 0%

profile of v1, /device:TPU:0, one launch (start us, length us, event | category | flops | bytes accessed | tf_op | source)
XLA Modules:
  0.0 478.6 jit_solution(4006321101818469535)
XLA Ops:
  4.8 7.3 %all-to-all-start = ((bf16[64,32,128]{2,0,1:T(8,128)(2,1)}), bf16[64,32,128]{2,0,1:T(8,128)(2,1)S(1)}, u32[]{:S(2)}, u32[]{:S(2)}) async-start(bf16[64,32,128]{2,0,1:T(8,128)(2,1)} %select_bitcast_fusion.8), calls=%async_computation | async-start | bytes 1048576 | tf_op jit(solution)/shard_map/all_to_all | solution.py:39
  25.2 5.4 %fusion.72 = bf16[64,96,128]{2,0,1:T(8,128)(2,1)} fusion(bf16[96,64,128]{2,1,0:T(8,128)(2,1)S(1)} %copy-done.59, pred[96]{0:T(512)(128)(4,1)S(1)} %get-tuple-element.12, bf16[96,2,128,128]{3,2,1,0:T(8,128)(2,1)} %param.16), kind=kOutput, calls=%fused_computation.101 | convolution fusion | flops 202113024 | bytes 6291552 | tf_op jit(solution)/shard_map/kej,eij->kei/dot_general | solution.py:46
  40.6 6.1 %all-to-all-start.1 = ((bf16[64,32,128]{2,0,1:T(8,128)(2,1)}), bf16[64,32,128]{2,0,1:T(8,128)(2,1)}, u32[]{:S(2)}, u32[]{:S(2)}) async-start(bf16[64,32,128]{2,0,1:T(8,128)(2,1)} %select_bitcast_fusion.7), calls=%async_computation.1 | async-start | bytes 1048576 | tf_op jit(solution)/shard_map/all_to_all | solution.py:39
  46.8 4.6 fusion.81
  57.2 5.3 %fusion.78 = bf16[64,96,128]{2,0,1:T(8,128)(2,1)} fusion(bf16[96,64,128]{2,1,0:T(8,128)(2,1)S(1)} %copy-done.60, pred[96]{0:T(512)(128)(4,1)S(1)} %get-tuple-element.12, bf16[96,2,128,128]{3,2,1,0:T(8,128)(2,1)} %param.16), kind=kOutput, calls=%fused_computation.103 | convolution fusion | flops 202113024 | bytes 6291552 | tf_op jit(solution)/shard_map/kej,eij->kei/dot_general | solution.py:46
  74.5 6.3 %all-to-all-start.2 = ((bf16[64,32,128]{2,0,1:T(8,128)(2,1)}), bf16[64,32,128]{2,0,1:T(8,128)(2,1)}, u32[]{:S(2)}, u32[]{:S(2)}) async-start(bf16[64,32,128]{2,0,1:T(8,128)(2,1)} %select_bitcast_fusion.6), calls=%async_computation.2 | async-start | bytes 1048576 | tf_op jit(solution)/shard_map/all_to_all | solution.py:39
  92.3 5.3 %fusion.84 = bf16[64,96,128]{2,0,1:T(8,128)(2,1)} fusion(bf16[96,64,128]{2,1,0:T(8,128)(2,1)S(1)} %copy-done.61, pred[96]{0:T(512)(128)(4,1)S(1)} %get-tuple-element.12, bf16[96,2,128,128]{3,2,1,0:T(8,128)(2,1)} %param.16), kind=kOutput, calls=%fused_computation.105 | convolution fusion | flops 202113024 | bytes 6291552 | tf_op jit(solution)/shard_map/kej,eij->kei/dot_general | solution.py:46
  111.5 6.3 %all-to-all-start.3 = ((bf16[64,32,128]{2,0,1:T(8,128)(2,1)}), bf16[64,32,128]{2,0,1:T(8,128)(2,1)}, u32[]{:S(2)}, u32[]{:S(2)}) async-start(bf16[64,32,128]{2,0,1:T(8,128)(2,1)} %select_bitcast_fusion.5), calls=%async_computation.3 | async-start | bytes 1048576 | tf_op jit(solution)/shard_map/all_to_all | solution.py:39
  125.2 5.3 %fusion.90 = bf16[64,96,128]{2,0,1:T(8,128)(2,1)} fusion(bf16[96,64,128]{2,1,0:T(8,128)(2,1)S(1)} %copy-done.56, pred[96]{0:T(512)(128)(4,1)S(1)} %get-tuple-element.12, bf16[96,2,128,128]{3,2,1,0:T(8,128)(2,1)} %param.16), kind=kOutput, calls=%fused_computation.107 | convolution fusion | flops 202113024 | bytes 6291552 | tf_op jit(solution)/shard_map/kej,eij->kei/dot_general | solution.py:46
  141.3 39.5 %psum.21 = f32[64,64]{0,1:T(8,128)S(1)} all-reduce(f32[64,64]{0,1:T(8,128)S(1)} %convolution_multiply_fusion.3), channel_id=1, replica_groups=mesh['dom'=32] {'dom'}, use_global_device_ids=true, to_apply=%region_0.3 | all-reduce | flops 4096 | bytes 32768 | tf_op jit(solution)/shard_map/psum | solution.py:67
  180.9 5.8 %cholesky.44 = f32[64,64]{1,0:T(8,128)S(1)} custom-call(f32[64,64]{1,0:T(8,128)S(1)} %fusion.301), custom_call_target="Cholesky" | custom-call | tf_op jit(solution)/shard_map/jit(cholesky)/cholesky | solution.py:68
  188.1 4.9 %custom-call.6 = f32[1,64,64]{1,2,0:T(8,128)S(1)} custom-call(f32[1,64,64]{2,1,0:T(8,128)S(1)} %fusion.296), custom_call_target="InvertDiagBlocksLowerTriangular" | custom-call | tf_op jit(solution)/shard_map/jit(_solve_triangular)/triangular_solve | solution.py:69
  214.7 5.3 %fusion.96 = bf16[64,96,128]{2,0,1:T(8,128)(2,1)} fusion(bf16[96,64,128]{2,1,0:T(8,128)(2,1)S(1)} %copy-done.62, pred[96]{0:T(512)(128)(4,1)S(1)} %get-tuple-element.12, bf16[96,2,128,128]{3,2,1,0:T(8,128)(2,1)} %param.16), kind=kOutput, calls=%fused_computation.109 | convolution fusion | flops 202113024 | bytes 6291552 | tf_op jit(solution)/shard_map/kej,eij->kei/dot_general | solution.py:46
  227.0 40.7 %psum.22 = f32[64,64]{0,1:T(8,128)S(1)} all-reduce(f32[64,64]{0,1:T(8,128)S(1)} %convolution_multiply_fusion.2), channel_id=1, replica_groups=mesh['dom'=32] {'dom'}, use_global_device_ids=true, to_apply=%region_3.8 | all-reduce | flops 4096 | bytes 32768 | tf_op jit(solution)/shard_map/psum | solution.py:84
  276.3 4.6 all-to-all-start.5
  291.4 5.3 %fusion.102 = bf16[64,96,128]{2,0,1:T(8,128)(2,1)} fusion(bf16[96,64,128]{2,1,0:T(8,128)(2,1)S(1)} %copy-done.63, pred[96]{0:T(512)(128)(4,1)S(1)} %get-tuple-element.12, bf16[96,2,128,128]{3,2,1,0:T(8,128)(2,1)} %param.16), kind=kOutput, calls=%fused_computation.111 | convolution fusion | flops 202113024 | bytes 6291552 | tf_op jit(solution)/shard_map/kej,eij->kei/dot_general | solution.py:46
  308.6 6.1 %all-to-all-start.6 = ((bf16[64,32,128]{2,0,1:T(8,128)(2,1)}), bf16[64,32,128]{2,0,1:T(8,128)(2,1)}, u32[]{:S(2)}, u32[]{:S(2)}) async-start(bf16[64,32,128]{2,0,1:T(8,128)(2,1)} %select_bitcast_fusion.2), calls=%async_computation.6 | async-start | bytes 1048576 | tf_op jit(solution)/shard_map/all_to_all | solution.py:39
  326.3 5.3 %fusion.108 = bf16[64,96,128]{2,0,1:T(8,128)(2,1)} fusion(bf16[96,64,128]{2,1,0:T(8,128)(2,1)S(1)} %copy-done.64, pred[96]{0:T(512)(128)(4,1)S(1)} %get-tuple-element.12, bf16[96,2,128,128]{3,2,1,0:T(8,128)(2,1)} %param.16), kind=kOutput, calls=%fused_computation.113 | convolution fusion | flops 202113024 | bytes 6291552 | tf_op jit(solution)/shard_map/kej,eij->kei/dot_general | solution.py:46
  345.4 6.5 %all-to-all-start.7 = ((bf16[64,32,128]{2,0,1:T(8,128)(2,1)}), bf16[64,32,128]{2,0,1:T(8,128)(2,1)}, u32[]{:S(2)}, u32[]{:S(2)}) async-start(bf16[64,32,128]{2,0,1:T(8,128)(2,1)} %select_bitcast_fusion.1), calls=%async_computation.7 | async-start | bytes 1048576 | tf_op jit(solution)/shard_map/all_to_all | solution.py:39
  359.3 5.3 %fusion.114 = bf16[64,96,128]{2,0,1:T(8,128)(2,1)} fusion(bf16[96,64,128]{2,1,0:T(8,128)(2,1)S(1)} %copy-done.57, pred[96]{0:T(512)(128)(4,1)S(1)} %get-tuple-element.12, bf16[96,2,128,128]{3,2,1,0:T(8,128)(2,1)} %param.16), kind=kOutput, calls=%fused_computation.115 | convolution fusion | flops 202113024 | bytes 6291552 | tf_op jit(solution)/shard_map/kej,eij->kei/dot_general | solution.py:46
  375.4 39.2 %psum.23 = f32[64,64]{0,1:T(8,128)S(1)} all-reduce(f32[64,64]{0,1:T(8,128)S(1)} %convolution_multiply_fusion.1), channel_id=1, replica_groups=mesh['dom'=32] {'dom'}, use_global_device_ids=true, to_apply=%region_5.10 | all-reduce | flops 4096 | bytes 32768 | tf_op jit(solution)/shard_map/psum | solution.py:67
  414.7 5.8 %cholesky.55 = f32[64,64]{1,0:T(8,128)S(1)} custom-call(f32[64,64]{1,0:T(8,128)S(1)} %fusion.299), custom_call_target="Cholesky" | custom-call | tf_op jit(solution)/shard_map/jit(cholesky)/cholesky | solution.py:68
  421.9 4.9 %custom-call.7 = f32[1,64,64]{1,2,0:T(8,128)S(1)} custom-call(f32[1,64,64]{2,1,0:T(8,128)S(1)} %fusion.297), custom_call_target="InvertDiagBlocksLowerTriangular" | custom-call | tf_op jit(solution)/shard_map/jit(_solve_triangular)/triangular_solve | solution.py:69
  448.4 5.3 %fusion.120 = bf16[64,96,128]{2,0,1:T(8,128)(2,1)} fusion(bf16[96,64,128]{2,1,0:T(8,128)(2,1)S(1)} %copy-done.58, pred[96]{0:T(512)(128)(4,1)S(1)} %get-tuple-element.12, bf16[96,2,128,128]{3,2,1,0:T(8,128)(2,1)} %param.16), kind=kOutput, calls=%fused_computation.117 | convolution fusion | flops 202113024 | bytes 6291552 | tf_op jit(solution)/shard_map/kej,eij->kei/dot_general | solution.py:46
  (291 shorter events, 238.7 us)
Async XLA Ops:
  0.6 20.7 %copy-start = (bf16[32,128,128]{2,1,0:T(8,128)(2,1)S(1)}, bf16[32,128,128]{2,1,0:T(8,128)(2,1)}, u32[]{:S(2)}) copy-start(bf16[32,128,128]{2,1,0:T(8,128)(2,1)} %param.15) | copy-start | bytes 3145732
  3.3 8.9 %copy-start.66 = (s32[1,96,2]{1,2,0:T(2,128)S(1)}, s32[1,96,2]{1,2,0:T(2,128)}, u32[]{:S(2)}) copy-start(s32[1,96,2]{1,2,0:T(2,128)} %param.19) | copy-start | bytes 2308
  4.8 25.8 %all-to-all-start = ((bf16[64,32,128]{2,0,1:T(8,128)(2,1)}), bf16[64,32,128]{2,0,1:T(8,128)(2,1)S(1)}, u32[]{:S(2)}, u32[]{:S(2)}) async-start(bf16[64,32,128]{2,0,1:T(8,128)(2,1)} %select_bitcast_fusion.8), calls=%async_computation | async-start | bytes 1048576 | tf_op jit(solution)/shard_map/all_to_all | solution.py:39
  25.2 5.4 %copy-start.1 = (bf16[32,128,128]{2,1,0:T(8,128)(2,1)S(1)}, bf16[32,128,128]{2,1,0:T(8,128)(2,1)}, u32[]{:S(2)}) copy-start(bf16[32,128,128]{2,1,0:T(8,128)(2,1)} %param.17) | copy-start | bytes 3145732
  40.6 21.9 %all-to-all-start.1 = ((bf16[64,32,128]{2,0,1:T(8,128)(2,1)}), bf16[64,32,128]{2,0,1:T(8,128)(2,1)}, u32[]{:S(2)}, u32[]{:S(2)}) async-start(bf16[64,32,128]{2,0,1:T(8,128)(2,1)} %select_bitcast_fusion.7), calls=%async_computation.1 | async-start | bytes 1048576 | tf_op jit(solution)/shard_map/all_to_all | solution.py:39
  74.5 23.2 %all-to-all-start.2 = ((bf16[64,32,128]{2,0,1:T(8,128)(2,1)}), bf16[64,32,128]{2,0,1:T(8,128)(2,1)}, u32[]{:S(2)}, u32[]{:S(2)}) async-start(bf16[64,32,128]{2,0,1:T(8,128)(2,1)} %select_bitcast_fusion.6), calls=%async_computation.2 | async-start | bytes 1048576 | tf_op jit(solution)/shard_map/all_to_all | solution.py:39
  87.3 3.0 copy-start.52
  101.4 2.1 copy-start.5
  111.5 21.9 %all-to-all-start.3 = ((bf16[64,32,128]{2,0,1:T(8,128)(2,1)}), bf16[64,32,128]{2,0,1:T(8,128)(2,1)}, u32[]{:S(2)}, u32[]{:S(2)}) async-start(bf16[64,32,128]{2,0,1:T(8,128)(2,1)} %select_bitcast_fusion.5), calls=%async_computation.3 | async-start | bytes 1048576 | tf_op jit(solution)/shard_map/all_to_all | solution.py:39
  121.2 2.1 copy-start.6
  194.9 74.2 %copy-start.2 = (bf16[64,4096]{1,0:T(8,128)(2,1)}, bf16[64,4096]{1,0:T(8,128)(2,1)S(1)}, u32[]{:S(2)}) copy-start(bf16[64,4096]{1,0:T(8,128)(2,1)S(1)} %convolution_convert_fusion.1) | copy-start | bytes 1572868
  200.3 19.7 %all-to-all-start.4 = ((bf16[64,32,128]{2,0,1:T(8,128)(2,1)}), bf16[64,32,128]{2,0,1:T(8,128)(2,1)}, u32[]{:S(2)}, u32[]{:S(2)}) async-start(bf16[64,32,128]{2,0,1:T(8,128)(2,1)} %select_bitcast_fusion.4), calls=%async_computation.4 | async-start | bytes 1048576 | tf_op jit(solution)/shard_map/all_to_all | solution.py:39
  276.3 20.4 %all-to-all-start.5 = ((bf16[64,32,128]{2,0,1:T(8,128)(2,1)}), bf16[64,32,128]{2,0,1:T(8,128)(2,1)}, u32[]{:S(2)}, u32[]{:S(2)}) async-start(bf16[64,32,128]{2,0,1:T(8,128)(2,1)} %select_bitcast_fusion.3), calls=%async_computation.5 | async-start | bytes 1048576 | tf_op jit(solution)/shard_map/all_to_all | solution.py:39
  308.6 23.0 %all-to-all-start.6 = ((bf16[64,32,128]{2,0,1:T(8,128)(2,1)}), bf16[64,32,128]{2,0,1:T(8,128)(2,1)}, u32[]{:S(2)}, u32[]{:S(2)}) async-start(bf16[64,32,128]{2,0,1:T(8,128)(2,1)} %select_bitcast_fusion.2), calls=%async_computation.6 | async-start | bytes 1048576 | tf_op jit(solution)/shard_map/all_to_all | solution.py:39
  321.3 3.0 copy-start.55
  335.3 2.1 copy-start.8
  345.4 22.1 %all-to-all-start.7 = ((bf16[64,32,128]{2,0,1:T(8,128)(2,1)}), bf16[64,32,128]{2,0,1:T(8,128)(2,1)}, u32[]{:S(2)}, u32[]{:S(2)}) async-start(bf16[64,32,128]{2,0,1:T(8,128)(2,1)} %select_bitcast_fusion.1), calls=%async_computation.7 | async-start | bytes 1048576 | tf_op jit(solution)/shard_map/all_to_all | solution.py:39
  428.6 30.0 %copy-start.17 = (bf16[64,4096]{1,0:T(8,128)(2,1)}, bf16[64,4096]{1,0:T(8,128)(2,1)S(1)}, u32[]{:S(2)}) copy-start(bf16[64,4096]{1,0:T(8,128)(2,1)S(1)} %convolution_convert_fusion) | copy-start | bytes 1572868
  434.1 19.7 %all-to-all-start.8 = ((bf16[64,32,128]{2,0,1:T(8,128)(2,1)}), bf16[64,32,128]{2,0,1:T(8,128)(2,1)}, u32[]{:S(2)}, u32[]{:S(2)}) async-start(bf16[64,32,128]{2,0,1:T(8,128)(2,1)} %select_bitcast_fusion), calls=%async_computation.8 | async-start | bytes 1048576 | tf_op jit(solution)/shard_map/all_to_all | solution.py:39
  459.8 1.3 collective-permute-start
  461.1 3.9 collective-permute-start.1
  465.0 3.9 collective-permute-start.2
  468.9 3.9 collective-permute-start.3
  472.9 4.8 %collective-permute-start.4 = (f32[64,64]{0,1:T(8,128)S(1)}, f32[64,64]{0,1:T(8,128)S(1)}, u32[]{:S(2)}, u32[]{:S(2)}) collective-permute-start(f32[64,64]{0,1:T(8,128)S(1)} %add.202), channel_id=1, source_target_pairs={{0,16},{1,17},{2,18},{3,19},{4,20},{5,21},{6,22},{7,23},{8,24},{9,... | collective-permute-start | bytes 49160 | tf_op jit(solution)/shard_map/ppermute | solution.py:88
  (57 other events, 91.0 us)
